TPU v7x, 32 devices: a whole 2x2x4 slice. The times are simulated.
32 devices in a mesh: crops: 2 (over y), rows: 4 (over x, core), cols: 4 (over z).
Axes of the slice: x: 2, y: 2, z: 4, core: 2. Of those that a mesh axis runs over, the one named last changes fastest.
Arguments:
- pair_maps: bfloat16 [2, 64, 1024, 1024], P('crops', None, 'rows', 'cols'), parts along dimension 0, may hold values from -6 to 6
- conv_a: bfloat16 [2, 3, 64, 192], replicated, may hold values from -0.25 to 0.25
- bias_a: float32 [2, 64], replicated, may hold values from -3 to 3
- conv_b: bfloat16 [2, 3, 64, 192], replicated, may hold values from -0.25 to 0.25
- bias_b: float32 [2, 64], replicated, may hold values from -3 to 3
- out_weight: bfloat16 [37, 64], replicated, may hold values from -3 to 3
- out_bias: float32 [37], replicated, may hold values from -4 to 4
Outputs:
- log_probs: float32 [2, 37, 1024, 1024], P('crops', None, ('rows', 'cols')), parts along dimension 0
There are 2 independent parts, one for each index of `crops`. A program takes and returns all parts, laid end to end along the dimension named above; an argument that names none is the same for every part. Nothing has to cross between parts.
All inputs are finite; a program needn't handle non-finite values.
Results may differ from a plain program's by a relative error of at most 0.0045.
Values may be sent and summed in bfloat16 or wider, within the bound.
No kernel may reach another device: no remote copies, remote signals or barrier semaphores. Data moves between devices by JAX's collectives and lax.ppermute only.
A program may use at most 192 MiB of HBM per device.

v0:
```python
import jax
import jax.numpy as jnp
from jax import lax
from jax.sharding import PartitionSpec as P

BLOCKS = 2
D1 = 4
D2 = 8


def padded(array, sides, width):
    for axis, dim in sides:
        peers, length = (lax.axis_size(axis), array.shape[dim])
        up = [(i, (i + 1) % peers) for i in range(peers - 1)]
        down = [(j, i) for i, j in up]
        last = lax.slice_in_dim(array, length - width, length, axis=dim)
        initial = lax.slice_in_dim(array, 0, width, axis=dim)
        before = lax.ppermute(last, axis, up)
        after = lax.ppermute(initial, axis, down)
        array = jnp.concatenate([before, array, after], axis=dim)
    return array


def dilated(widened, kernel, dilation):
    height = widened.shape[2] - 2 * dilation
    breadth = widened.shape[3] - 2 * dilation
    summed = None
    for tap_row in range(3):
        stacked = jnp.concatenate(
            [
                widened[
                    :,
                    :,
                    tap_row * dilation : tap_row * dilation + height,
                    tap_col * dilation : tap_col * dilation + breadth,
                ]
                for tap_col in range(3)
            ],
            axis=1,
        )
        partial_sum = jnp.einsum(
            "oc,nchw->nohw", kernel[tap_row], stacked, preferred_element_type=jnp.float32
        )
        summed = partial_sum if summed is None else summed + partial_sum
    return summed


def widen_each(field, width):
    return padded(field, (("rows", 2), ("cols", 3)), width)


def shards(pair_maps, conv_a, bias_a, conv_b, bias_b, out_weight, out_bias):
    field = pair_maps
    for block_index in range(BLOCKS):
        inner = jax.nn.elu(
            dilated(widen_each(field, D1), conv_a[block_index], D1)
            + bias_a[block_index][None, :, None, None]
        ).astype(jnp.bfloat16)
        field = (
            field.astype(jnp.float32)
            + dilated(widen_each(inner, D2), conv_b[block_index], D2)
            + bias_b[block_index][None, :, None, None]
        ).astype(jnp.bfloat16)
    logits = (
        jnp.einsum("kc,nchw->nkhw", out_weight, field, preferred_element_type=jnp.float32)
        + out_bias[None, :, None, None]
    ).astype(jnp.bfloat16)
    strips = lax.all_to_all(logits, "cols", split_axis=2, concat_axis=3, tiled=True)
    flipped = lax.all_to_all(strips, ("rows", "cols"), split_axis=3, concat_axis=2, tiled=True)
    mirrored = jnp.swapaxes(flipped, 2, 3)
    symmetric = (strips.astype(jnp.float32) + mirrored.astype(jnp.float32)) * 0.5
    return symmetric - jnp.log(jnp.sum(jnp.exp(symmetric), axis=1, keepdims=True))


def solution(mesh):
    in_specs = (P("crops", None, "rows", "cols"), P(), P(), P(), P(), P(), P())
    out_specs = P("crops", None, ("rows", "cols"), None)
    return jax.shard_map(shards, mesh=mesh, in_specs=in_specs, out_specs=out_specs, check_vma=False)
```

profile of v0, /device:TPU:0, one launch (start us, length us, event | category | flops | bytes accessed | tf_op | source)
XLA Modules:
  0.0 1072.0 jit_solution(16350415783186758611)
XLA Ops:
  0.0 11.5 %copy.17 = bf16[1,64,256,256]{3,1,2,0:T(8,128)(2,1)} copy(bf16[1,64,256,256]{3,2,1,0:T(8,128)(2,1)} %param.7) | data formatting | bytes 16777216 | tf_op args[0]
  17.0 11.5 %constant_dynamic-update-slice_fusion.1 = bf16[1,64,264,256]{3,1,2,0:T(8,128)(2,1)} fusion(bf16[1,64,264,256]{3,1,2,0:T(8,128)(2,1)} %constant_dynamic-update-slice_fusion.2, bf16[1,64,256,256]{3,2,1,0:T(8,128)(2,1)} %param.7), kind=kLoop, calls=%fused_computation.162 | loop fusion | bytes 16777216
  29.2 6.8 fusion.165
  36.0 6.1 copy.21
  42.2 6.1 copy.24
  49.6 5.2 collective-permute-start.2
  63.3 5.2 copy.25
  68.5 36.7 %fusion.99 = (bf16[1,64,256,256]{3,1,2,0:T(8,128)(2,1)}, bf16[1,64,256,256]{3,1,2,0:T(8,128)(2,1)}, bf16[1,64,256,256]{3,1,2,0:T(8,128)(2,1)}, bf16[1,64,256,256]{3,1,2,0:T(8,128)(2,1)}) fusion(bf16[1,64,264,256]{3,1,2,0:T(8,128)(2,1)} %constant_dynamic-update-slice_fusion, bf16[1,64,264,4]{3,1,2,0:T(8,128)(2,1)} %copy.22, bf16[1,64,264,4]{3,1,2,0:T(8,128)(2,1)} %copy.25), kind=kLoop, calls=%fused_computation.130 | loop fusion | flops 67108864 | bytes 42475520 | tf_op jit(solution)/shard_map/concatenate | solution.py:20
  105.2 16.8 %fusion.53 = f32[256,256,64]{1,2,0:T(8,128)} fusion(bf16[1,64,256,256]{3,1,2,0:T(8,128)(2,1)} %get-tuple-element.40, bf16[1,64,256,256]{3,1,2,0:T(8,128)(2,1)} %copy.17, bf16[1,64,256,256]{3,1,2,0:T(8,128)(2,1)} %get-tuple-element.23, bf16[2,3,64,192]{3,2,1,0:T(8,128)(2,1)S(1)} %copy-done.6), kind=kOutput, calls=%fused_computation.59 | convolution fusion | flops 1686110208 | bytes 41975808 | tf_op jit(solution)/shard_map/oc,nchw->nohw/dot_general | solution.py:41
  122.0 17.8 %fusion.48 = f32[256,256,64]{1,2,0:T(8,128)} fusion(bf16[1,64,256,256]{3,1,2,0:T(8,128)(2,1)} %copy.17, bf16[1,64,4,256]{3,1,2,0:T(8,128)(2,1)S(1)} %collective-permute-done, bf16[1,64,256,256]{3,1,2,0:T(8,128)(2,1)} %get-tuple-element.39, bf16[1,64,256,256]{3,1,2,0:T(8,128)(2,1)} %get-tuple-element.24, bf16[2,3,64,192]{3,2,1,0:T(8,128)(2,1)S(1)} %copy-done.6), kind=kOutput, calls=%fused_computation.54 | convolution fusion | flops 1711276032 | bytes 42106880 | tf_op jit(solution)/shard_map/oc,nchw->nohw/dot_general | solution.py:41
  139.9 34.6 %fusion.86 = bf16[1,64,256,256]{3,1,2,0:T(8,128)(2,1)} fusion(f32[256,256,64]{1,2,0:T(8,128)} %fusion.48, f32[256,256,64]{1,2,0:T(8,128)} %fusion.53, bf16[1,64,264,4]{3,1,2,0:T(8,128)(2,1)} %copy.25, bf16[1,64,264,256]{3,1,2,0:T(8,128)(2,1)} %constant_dynamic-update-slice_fusion, bf16[1,64,4,256]{3,1,2,0:T(8,128)(2,1)S(1)} %collective-permute-done.1, ...), kind=kOutput, calls=%fused_computation.97 | convolution fusion | flops 1790967808 | bytes 59417088 | tf_op jit(solution)/shard_map/oc,nchw->nohw/dot_general | solution.py:41
  186.9 5.9 fusion.163
  192.8 5.3 copy.28
  202.3 5.4 copy.30
  222.5 27.4 %maximum_maximum_fusion = (bf16[1,64,272,264]{3,1,2,0:T(8,128)(2,1)}, bf16[1,64,272,264]{3,1,2,0:T(8,128)(2,1)}) fusion(bf16[1,64,8,256]{3,1,2,0:T(8,128)(2,1)S(1)} %collective-permute-done.5, bf16[1,64,256,256]{3,1,2,0:T(8,128)(2,1)} %fusion.86, bf16[1,64,8,256]{3,1,2,0:T(8,128)(2,1)S(1)} %collective-permute-done.4, bf16[1,64,272,8]{3,1,2,0:T(8,128)(2,1)} %copy.29, ...), kind=kLoop, calls=%fused_computation.116 | loop fusion | flops 73531392 | bytes 27852800 | tf_op jit(solution)/shard_map/concatenate | solution.py:20
  249.9 17.9 %fusion.158 = (bf16[1,64,256,256]{3,1,2,0:T(8,128)(2,1)}, bf16[1,64,256,256]{3,1,2,0:T(8,128)(2,1)}, bf16[1,64,256,256]{3,1,2,0:T(8,128)(2,1)}) fusion(bf16[1,64,272,264]{3,1,2,0:T(8,128)(2,1)} %get-tuple-element.31), kind=kLoop, calls=%fused_computation.182 | loop fusion | bytes 50331648 | tf_op jit(solution)/shard_map/slice | solution.py:31
  270.6 16.4 %fusion.159 = (bf16[1,64,256,256]{3,1,2,0:T(8,128)(2,1)}, bf16[1,64,256,256]{3,1,2,0:T(8,128)(2,1)}, bf16[1,64,256,256]{3,1,2,0:T(8,128)(2,1)}) fusion(bf16[1,64,272,264]{3,1,2,0:T(8,128)(2,1)S(1)} %bitcast.211), kind=kLoop, calls=%fused_computation.183 | loop fusion | bytes 50331648 | tf_op jit(solution)/shard_map/slice | solution.py:31
  287.0 16.8 %fusion.60 = f32[256,256,64]{1,2,0:T(8,128)} fusion(bf16[1,64,256,256]{3,1,2,0:T(8,128)(2,1)} %get-tuple-element.15, bf16[1,64,256,256]{3,1,2,0:T(8,128)(2,1)} %fusion.86, bf16[1,64,256,256]{3,1,2,0:T(8,128)(2,1)} %get-tuple-element.12, bf16[2,3,64,192]{3,2,1,0:T(8,128)(2,1)S(1)} %copy-done.8), kind=kOutput, calls=%fused_computation.67 | convolution fusion | flops 1686110208 | bytes 41975808 | tf_op jit(solution)/shard_map/oc,nchw->nohw/dot_general | solution.py:41
  303.8 18.6 %fusion.33 = f32[256,256,64]{1,2,0:T(8,128)} fusion(bf16[1,64,256,256]{3,1,2,0:T(8,128)(2,1)} %fusion.86, bf16[1,64,8,256]{3,1,2,0:T(8,128)(2,1)S(1)} %collective-permute-done.4, bf16[1,64,256,256]{3,1,2,0:T(8,128)(2,1)} %get-tuple-element.16, bf16[1,64,256,256]{3,1,2,0:T(8,128)(2,1)} %get-tuple-element.13, bf16[2,3,64,192]{3,2,1,0:T(8,128)(2,1)S(1)} %copy-done.8), kind=kOutput, calls=%fused_computation.38 | convolution fusion | flops 1711276032 | bytes 42237952 | tf_op jit(solution)/shard_map/oc,nchw->nohw/dot_general | solution.py:41
  322.4 42.8 %fusion.92 = bf16[1,64,256,256]{3,1,2,0:T(8,128)(2,1)} fusion(f32[256,256,64]{1,2,0:T(8,128)} %fusion.33, f32[256,256,64]{1,2,0:T(8,128)} %fusion.60, f32[64]{0:T(128)S(1)} %get-tuple-element.52, bf16[1,64,8,256]{3,1,2,0:T(8,128)(2,1)S(1)} %collective-permute-done.5, bf16[1,64,256,256]{3,1,2,0:T(8,128)(2,1)} %fusion.86, ...), kind=kOutput, calls=%fused_computation.105 | convolution fusion | flops 1736441856 | bytes 75792896 | tf_op jit(solution)/shard_map/oc,nchw->nohw/dot_general | solution.py:41
  367.5 6.4 collective-permute-start.8
  384.6 6.1 copy.32
  394.7 6.2 copy.34
  413.5 25.8 %maximum_maximum_fusion.2 = (bf16[1,64,264,260]{3,1,2,0:T(8,128)(2,1)}, bf16[1,64,264,260]{3,1,2,0:T(8,128)(2,1)}) fusion(bf16[1,64,4,256]{3,1,2,0:T(8,128)(2,1)S(1)} %collective-permute-done.9, bf16[1,64,256,256]{3,1,2,0:T(8,128)(2,1)} %fusion.92, bf16[1,64,4,256]{3,1,2,0:T(8,128)(2,1)S(1)} %collective-permute-done.8, bf16[1,64,264,4]{3,1,2,0:T(8,128)(2,1)} %copy.33, ...), kind=kLoop, calls=%fused_computation.121 | loop fusion | flops 70287360 | bytes 26492928 | tf_op jit(solution)/shard_map/concatenate | solution.py:20
  439.3 18.1 %fusion.160 = (bf16[1,64,256,256]{3,1,2,0:T(8,128)(2,1)}, bf16[1,64,256,256]{3,1,2,0:T(8,128)(2,1)}, bf16[1,64,256,256]{3,1,2,0:T(8,128)(2,1)}) fusion(bf16[1,64,264,260]{3,1,2,0:T(8,128)(2,1)} %get-tuple-element.35), kind=kLoop, calls=%fused_computation.184 | loop fusion | bytes 50331648 | tf_op jit(solution)/shard_map/slice | solution.py:31
  460.1 16.4 %fusion.161 = (bf16[1,64,256,256]{3,1,2,0:T(8,128)(2,1)}, bf16[1,64,256,256]{3,1,2,0:T(8,128)(2,1)}, bf16[1,64,256,256]{3,1,2,0:T(8,128)(2,1)}) fusion(bf16[1,64,264,260]{3,1,2,0:T(8,128)(2,1)S(1)} %bitcast.209), kind=kLoop, calls=%fused_computation.185 | loop fusion | bytes 50331648 | tf_op jit(solution)/shard_map/slice | solution.py:31
  476.4 16.8 %fusion.69 = f32[256,256,64]{1,2,0:T(8,128)} fusion(bf16[1,64,256,256]{3,1,2,0:T(8,128)(2,1)} %get-tuple-element.21, bf16[1,64,256,256]{3,1,2,0:T(8,128)(2,1)} %fusion.92, bf16[1,64,256,256]{3,1,2,0:T(8,128)(2,1)} %get-tuple-element.18, bf16[2,3,64,192]{3,2,1,0:T(8,128)(2,1)S(1)} %copy-done.7), kind=kOutput, calls=%fused_computation.77 | convolution fusion | flops 1686110208 | bytes 41975808 | tf_op jit(solution)/shard_map/oc,nchw->nohw/dot_general | solution.py:41
  493.3 18.0 %fusion.21 = f32[256,256,64]{1,2,0:T(8,128)} fusion(bf16[1,64,256,256]{3,1,2,0:T(8,128)(2,1)} %fusion.92, bf16[1,64,4,256]{3,1,2,0:T(8,128)(2,1)S(1)} %collective-permute-done.8, bf16[1,64,256,256]{3,1,2,0:T(8,128)(2,1)} %get-tuple-element.22, bf16[1,64,256,256]{3,1,2,0:T(8,128)(2,1)} %get-tuple-element.19, bf16[2,3,64,192]{3,2,1,0:T(8,128)(2,1)S(1)} %copy-done.7), kind=kOutput, calls=%fused_computation.26 | convolution fusion | flops 1711276032 | bytes 42106880 | tf_op jit(solution)/shard_map/oc,nchw->nohw/dot_general | solution.py:41
  511.3 35.8 %fusion.88 = bf16[1,64,256,256]{3,1,2,0:T(8,128)(2,1)} fusion(f32[256,256,64]{1,2,0:T(8,128)} %fusion.21, f32[256,256,64]{1,2,0:T(8,128)} %fusion.69, f32[64]{0:T(128)S(1)} %copy-done.5, bf16[1,64,4,256]{3,1,2,0:T(8,128)(2,1)S(1)} %collective-permute-done.9, bf16[1,64,256,256]{3,1,2,0:T(8,128)(2,1)} %fusion.92, ...), kind=kOutput, calls=%fused_computation.99 | convolution fusion | flops 1740636160 | bytes 67273216 | tf_op jit(solution)/shard_map/oc,nchw->nohw/dot_general | solution.py:41
  554.3 5.5 collective-permute-done.13
  564.6 5.9 fusion.162
  570.6 5.3 copy.36
  579.4 5.4 copy.38
  600.1 27.4 %maximum_maximum_fusion.1 = (bf16[1,64,272,264]{3,1,2,0:T(8,128)(2,1)}, bf16[1,64,272,264]{3,1,2,0:T(8,128)(2,1)}) fusion(bf16[1,64,8,256]{3,1,2,0:T(8,128)(2,1)S(1)} %collective-permute-done.13, bf16[1,64,256,256]{3,1,2,0:T(8,128)(2,1)} %fusion.88, bf16[1,64,8,256]{3,1,2,0:T(8,128)(2,1)S(1)} %collective-permute-done.12, bf16[1,64,272,8]{3,1,2,0:T(8,128)(2,1)} %copy.37, ...), kind=kLoop, calls=%fused_computation.118 | loop fusion | flops 73531392 | bytes 27852800 | tf_op jit(solution)/shard_map/concatenate | solution.py:20
  627.5 18.1 %fusion.156 = (bf16[1,64,256,256]{3,1,2,0:T(8,128)(2,1)}, bf16[1,64,256,256]{3,1,2,0:T(8,128)(2,1)}, bf16[1,64,256,256]{3,1,2,0:T(8,128)(2,1)}) fusion(bf16[1,64,272,264]{3,1,2,0:T(8,128)(2,1)} %get-tuple-element.27), kind=kLoop, calls=%fused_computation.180 | loop fusion | bytes 50331648 | tf_op jit(solution)/shard_map/slice | solution.py:31
  648.4 16.4 %fusion.157 = (bf16[1,64,256,256]{3,1,2,0:T(8,128)(2,1)}, bf16[1,64,256,256]{3,1,2,0:T(8,128)(2,1)}, bf16[1,64,256,256]{3,1,2,0:T(8,128)(2,1)}) fusion(bf16[1,64,272,264]{3,1,2,0:T(8,128)(2,1)S(1)} %bitcast.213), kind=kLoop, calls=%fused_computation.181 | loop fusion | bytes 50331648 | tf_op jit(solution)/shard_map/slice | solution.py:31
  664.8 21.5 %fusion.3 = f32[256,256,64]{1,2,0:T(8,128)} fusion(bf16[1,64,8,256]{3,1,2,0:T(8,128)(2,1)S(1)} %collective-permute-done.13, bf16[1,64,256,256]{3,1,2,0:T(8,128)(2,1)} %fusion.88, bf16[1,64,256,256]{3,1,2,0:T(8,128)(2,1)} %get-tuple-element.9, bf16[1,64,256,256]{3,1,2,0:T(8,128)(2,1)} %get-tuple-element.6, bf16[2,3,64,192]{3,2,1,0:T(8,128)(2,1)S(1)} %copy-done.9), kind=kOutput, calls=%fused_computation.8 | convolution fusion | flops 1711276032 | bytes 42237952 | tf_op jit(solution)/shard_map/oc,nchw->nohw/dot_general | solution.py:41
  686.3 18.4 %fusion.9 = f32[256,256,64]{1,2,0:T(8,128)} fusion(bf16[1,64,256,256]{3,1,2,0:T(8,128)(2,1)} %fusion.88, bf16[1,64,8,256]{3,1,2,0:T(8,128)(2,1)S(1)} %collective-permute-done.12, bf16[1,64,256,256]{3,1,2,0:T(8,128)(2,1)} %get-tuple-element.10, bf16[1,64,256,256]{3,1,2,0:T(8,128)(2,1)} %get-tuple-element.7, bf16[2,3,64,192]{3,2,1,0:T(8,128)(2,1)S(1)} %copy-done.9), kind=kOutput, calls=%fused_computation.14 | convolution fusion | flops 1711276032 | bytes 42237952 | tf_op jit(solution)/shard_map/oc,nchw->nohw/dot_general | solution.py:41
  704.7 24.7 %fusion.105 = bf16[1,37,256,256]{3,1,0,2:T(8,128)(2,1)} fusion(f32[37]{0:T(128)S(1)} %copy-done.10, f32[256,256,64]{1,2,0:T(8,128)} %fusion.3, f32[256,256,64]{1,2,0:T(8,128)} %fusion.9, bf16[1,64,256,256]{3,1,2,0:T(8,128)(2,1)} %fusion.92, f32[64]{0:T(128)S(1)} %copy-done.4, bf16[1,64,256,256]{3,1,2,0:T(8,128)(2,1)} %get-tuple-element.8, ...), kind=kOutput, calls=%fused_computation.135 | convolution fusion | flops 2026504192 | bytes 72002560 | tf_op jit(solution)/shard_map/kc,nchw->nkhw/dot_general | solution.py:65
  729.4 121.8 %all_to_all.27 = bf16[1,37,256,256]{3,1,0,2:T(8,128)(2,1)} all-to-all(bf16[1,37,256,256]{3,1,0,2:T(8,128)(2,1)} %fusion.105), channel_id=1, replica_groups=mesh['crops'=2,'rows'=4,'cols'=4] {'cols'}, dimensions={2} | all-to-all | bytes 9699328 | tf_op jit(solution)/shard_map/all_to_all | solution.py:68
  851.2 13.0 %copy.41 = bf16[1,37,64,4,256]{2,1,4,3,0:T(8,128)(2,1)} copy(bf16[1,37,64,4,256]{4,1,2,3,0:T(8,128)(2,1)} %bitcast.215) | data formatting | bytes 9699328 | tf_op jit(solution)/shard_map/all_to_all | solution.py:68
  864.3 14.8 %reshape.152 = bf16[16,2,75776]{2,1,0:T(2,128)(2,1)} reshape(bf16[1024,1,37,64]{3,2,1,0:T(8,128)(2,1)} %bitcast.205) | data formatting | bytes 9699328
  879.0 113.2 %all_to_all.28 = bf16[16,2,75776]{2,1,0:T(2,128)(2,1)} all-to-all(bf16[16,2,75776]{2,1,0:T(2,128)(2,1)} %reshape.152), channel_id=1, replica_groups=mesh['crops'=2,'rows'=4,'cols'=4] {'rows','cols'}, dimensions={0} | all-to-all | bytes 9699328 | tf_op jit(solution)/shard_map/all_to_all | solution.py:69
  992.2 16.0 %reshape.153 = bf16[1024,1,37,64]{3,2,1,0:T(8,128)(2,1)} reshape(bf16[16,2,75776]{2,1,0:T(2,128)(2,1)} %all_to_all.28) | data formatting | bytes 9699328
  1008.2 18.3 %copy.42 = f32[1,37,64,16,64]{4,1,2,3,0:T(8,128)} copy(bf16[1,37,64,16,64]{2,1,4,3,0:T(8,128)(2,1)} %bitcast.214) | data formatting | bytes 14548992 | tf_op jit(solution)/shard_map/convert_element_type | solution.py:71
  1026.4 15.4 %exponential_reduce_fusion = f32[64,1024]{0,1:T(8,128)S(1)} fusion(f32[1,37,64,1024]{2,1,0,3:T(8,128)} %bitcast.203, bf16[1,37,64,1024]{2,1,0,3:T(8,128)(2,1)} %bitcast.206), kind=kLoop, calls=%fused_computation.94 | loop fusion | flops 9633792 | bytes 14811136 | tf_op jit(solution)/shard_map/reduce_sum | solution.py:72
  1042.7 13.6 %fusion.93 = f32[1,37,64,1024]{2,1,0,3:T(8,128)} fusion(f32[1,37,64,1024]{2,1,0,3:T(8,128)S(1)} %bitcast.204, bf16[1,37,64,1024]{2,1,0,3:T(8,128)(2,1)} %bitcast.207, f32[64,1024]{0,1:T(8,128)S(1)} %log.8), kind=kLoop, calls=%fused_computation.120 | loop fusion | flops 9699328 | bytes 24510464 | tf_op jit(solution)/shard_map/sub | solution.py:72
  1056.2 15.6 %copy.43 = f32[1,37,64,1024]{3,2,1,0:T(8,128)} copy(f32[1,37,64,1024]{2,1,0,3:T(8,128)} %fusion.93) | data formatting | bytes 19398656 | tf_op jit(solution)/shard_map/sub | solution.py:72
  (98 shorter events, 116.6 us)
Async XLA Ops:
  0.0 704.7 %copy-start = (bf16[37,64]{1,0:T(8,128)(2,1)S(1)}, bf16[37,64]{1,0:T(8,128)(2,1)}, u32[]{:S(2)}) copy-start(bf16[37,64]{1,0:T(8,128)(2,1)} %param.12) | copy-start | bytes 14212
  12.5 3.9 collective-permute-start
  14.9 13.7 %collective-permute-start.1 = (bf16[1,64,4,256]{3,1,2,0:T(8,128)(2,1)S(1)}, bf16[1,64,4,256]{3,1,2,0:T(8,128)(2,1)S(1)}, u32[]{:S(2)}, u32[]{:S(2)}) collective-permute-start(bf16[1,64,4,256]{3,1,2,0:T(8,128)(2,1)S(1)} %get-tuple-element.49), channel_id=1, source_target_pairs={{4,0},{8,4},{12,8},{5,1},{9,5},{13,9},{6,2},{10,6},{14,10},{7,3},{... | collective-permute-start | bytes 393224 | tf_op jit(solution)/shard_map/ppermute | solution.py:19
  28.6 26.2 %copy-start.2 = (f32[2,64]{1,0:T(2,128)S(1)}, f32[2,64]{1,0:T(2,128)}, u32[]{:S(2)}) copy-start(f32[2,64]{1,0:T(2,128)} %param.9) | copy-start | bytes 1540
  48.3 15.0 %collective-permute-start.3 = (bf16[1,64,264,4]{2,1,3,0:T(8,128)(2,1)S(1)}, bf16[1,64,264,4]{2,1,3,0:T(8,128)(2,1)S(1)}, u32[]{:S(2)}, u32[]{:S(2)}) collective-permute-start(bf16[1,64,264,4]{2,1,3,0:T(8,128)(2,1)S(1)} %copy.24), channel_id=1, source_target_pairs={{1,0},{2,1},{3,2},{5,4},{6,5},{7,6},{9,8},{10,9},{11,10},{13,12},{... | collective-permute-start | bytes 405512 | tf_op jit(solution)/shard_map/ppermute | solution.py:19
  49.6 8.6 collective-permute-start.2
  68.5 36.7 %copy-start.6 = (bf16[2,3,64,192]{3,2,1,0:T(8,128)(2,1)S(1)}, bf16[2,3,64,192]{3,2,1,0:T(8,128)(2,1)}, u32[]{:S(2)}) copy-start(bf16[2,3,64,192]{3,2,1,0:T(8,128)(2,1)} %param.8) | copy-start | bytes 442372
  175.6 5.6 collective-permute-start.5
  176.9 5.4 collective-permute-start.4
  186.9 22.1 %copy-start.3 = (f32[2,64]{1,0:T(2,128)S(1)}, f32[2,64]{1,0:T(2,128)}, u32[]{:S(2)}) copy-start(f32[2,64]{1,0:T(2,128)} %param.11) | copy-start | bytes 1540
  198.2 11.4 %collective-permute-start.6 = (bf16[1,64,272,8]{2,3,1,0:T(8,128)(2,1)S(1)}, bf16[1,64,272,8]{2,3,1,0:T(8,128)(2,1)S(1)}, u32[]{:S(2)}, u32[]{:S(2)}) collective-permute-start(bf16[1,64,272,8]{2,3,1,0:T(8,128)(2,1)S(1)} %copy.28), channel_id=1, source_target_pairs={{0,1},{1,2},{2,3},{4,5},{5,6},{6,7},{8,9},{9,10},{10,11},{12,13},{... | collective-permute-start | bytes 835592 | tf_op jit(solution)/shard_map/ppermute | solution.py:18
  207.6 9.8 collective-permute-start.7
  249.9 18.0 %slice-start.4 = ((s8[13369344]{0:T(1024)(128)(4,1)}), s8[4194304]{0:T(1024)(128)(4,1)S(1)}, s32[]{:S(2)}) async-start(s8[13369344]{0:T(1024)(128)(4,1)} %bitcast.210), calls=%async_computation.6 | async-start | bytes 8388608
  249.9 19.4 %slice-start.5 = ((s8[13369344]{0:T(1024)(128)(4,1)}), s8[4194304]{0:T(1024)(128)(4,1)S(1)}, s32[]{:S(2)}) async-start(s8[13369344]{0:T(1024)(128)(4,1)} %bitcast.210), calls=%async_computation.7 | async-start | bytes 8388608
  249.9 20.6 %slice-start.6 = ((s8[13369344]{0:T(1024)(128)(4,1)}), s8[4194304]{0:T(1024)(128)(4,1)S(1)}, s32[]{:S(2)}) async-start(s8[13369344]{0:T(1024)(128)(4,1)} %bitcast.210), calls=%async_computation.8 | async-start | bytes 8388608
  249.9 20.7 %slice-start.7 = ((s8[13369344]{0:T(1024)(128)(4,1)}), s8[786432]{0:T(1024)(128)(4,1)S(1)}, s32[]{:S(2)}) async-start(s8[13369344]{0:T(1024)(128)(4,1)} %bitcast.210), calls=%async_computation.9 | async-start | bytes 1572864
  270.6 16.4 %copy-start.8 = (bf16[2,3,64,192]{3,2,1,0:T(8,128)(2,1)S(1)}, bf16[2,3,64,192]{3,2,1,0:T(8,128)(2,1)}, u32[]{:S(2)}) copy-start(bf16[2,3,64,192]{3,2,1,0:T(8,128)(2,1)} %param.10) | copy-start | bytes 442372
  366.2 7.7 collective-permute-start.9
  367.5 7.4 collective-permute-start.8
  390.8 11.4 %collective-permute-start.10 = (bf16[1,64,264,4]{2,1,3,0:T(8,128)(2,1)S(1)}, bf16[1,64,264,4]{2,1,3,0:T(8,128)(2,1)S(1)}, u32[]{:S(2)}, u32[]{:S(2)}) collective-permute-start(bf16[1,64,264,4]{2,1,3,0:T(8,128)(2,1)S(1)} %copy.32), channel_id=1, source_target_pairs={{0,1},{1,2},{2,3},{4,5},{5,6},{6,7},{8,9},{9,10},{10,11},{12,13},{... | collective-permute-start | bytes 405512 | tf_op jit(solution)/shard_map/ppermute | solution.py:18
  400.8 7.6 collective-permute-start.11
  439.3 18.1 %slice-start = ((s8[12976128]{0:T(1024)(128)(4,1)}), s8[4194304]{0:T(1024)(128)(4,1)S(1)}, s32[]{:S(2)}) async-start(s8[12976128]{0:T(1024)(128)(4,1)} %bitcast.208), calls=%async_computation.2 | async-start | bytes 8388608
  439.3 19.5 %slice-start.1 = ((s8[12976128]{0:T(1024)(128)(4,1)}), s8[4194304]{0:T(1024)(128)(4,1)S(1)}, s32[]{:S(2)}) async-start(s8[12976128]{0:T(1024)(128)(4,1)} %bitcast.208), calls=%async_computation.3 | async-start | bytes 8388608
  439.3 20.7 %slice-start.2 = ((s8[12976128]{0:T(1024)(128)(4,1)}), s8[4194304]{0:T(1024)(128)(4,1)S(1)}, s32[]{:S(2)}) async-start(s8[12976128]{0:T(1024)(128)(4,1)} %bitcast.208), calls=%async_computation.4 | async-start | bytes 8388608
  439.3 20.7 %slice-start.3 = ((s8[12976128]{0:T(1024)(128)(4,1)}), s8[393216]{0:T(1024)(128)(4,1)S(1)}, s32[]{:S(2)}) async-start(s8[12976128]{0:T(1024)(128)(4,1)} %bitcast.208), calls=%async_computation.5 | async-start | bytes 786432
  460.1 16.4 %copy-start.7 = (bf16[2,3,64,192]{3,2,1,0:T(8,128)(2,1)S(1)}, bf16[2,3,64,192]{3,2,1,0:T(8,128)(2,1)}, u32[]{:S(2)}) copy-start(bf16[2,3,64,192]{3,2,1,0:T(8,128)(2,1)} %param.8) | copy-start | bytes 442372
  493.3 18.0 %copy-start.5 = (f32[64]{0:T(128)S(1)}, f32[64]{0:T(128)}, u32[]{:S(2)}) copy-start(f32[64]{0:T(128)} %get-tuple-element.53) | copy-start | bytes 772
  548.2 6.1 collective-permute-start.12
  553.0 6.8 collective-permute-start.13
  575.9 10.2 collective-permute-start.14
  584.8 10.4 collective-permute-start.15
  627.5 18.1 %slice-start.8 = ((s8[13369344]{0:T(1024)(128)(4,1)}), s8[4194304]{0:T(1024)(128)(4,1)S(1)}, s32[]{:S(2)}) async-start(s8[13369344]{0:T(1024)(128)(4,1)} %bitcast.212), calls=%async_computation.10 | async-start | bytes 8388608
  627.5 19.5 %slice-start.9 = ((s8[13369344]{0:T(1024)(128)(4,1)}), s8[4194304]{0:T(1024)(128)(4,1)S(1)}, s32[]{:S(2)}) async-start(s8[13369344]{0:T(1024)(128)(4,1)} %bitcast.212), calls=%async_computation.11 | async-start | bytes 8388608
  627.5 20.7 %slice-start.10 = ((s8[13369344]{0:T(1024)(128)(4,1)}), s8[4194304]{0:T(1024)(128)(4,1)S(1)}, s32[]{:S(2)}) async-start(s8[13369344]{0:T(1024)(128)(4,1)} %bitcast.212), calls=%async_computation.12 | async-start | bytes 8388608
  627.5 20.8 %slice-start.11 = ((s8[13369344]{0:T(1024)(128)(4,1)}), s8[786432]{0:T(1024)(128)(4,1)S(1)}, s32[]{:S(2)}) async-start(s8[13369344]{0:T(1024)(128)(4,1)} %bitcast.212), calls=%async_computation.13 | async-start | bytes 1572864
  648.4 16.4 %copy-start.9 = (bf16[2,3,64,192]{3,2,1,0:T(8,128)(2,1)S(1)}, bf16[2,3,64,192]{3,2,1,0:T(8,128)(2,1)}, u32[]{:S(2)}) copy-start(bf16[2,3,64,192]{3,2,1,0:T(8,128)(2,1)} %param.10) | copy-start | bytes 442372
  686.3 18.4 %copy-start.4 = (f32[64]{0:T(128)S(1)}, f32[64]{0:T(128)}, u32[]{:S(2)}) copy-start(f32[64]{0:T(128)} %get-tuple-element.51) | copy-start | bytes 772
  686.3 18.4 %copy-start.10 = (f32[37]{0:T(128)S(1)}, f32[37]{0:T(128)}, u32[]{:S(2)}) copy-start(f32[37]{0:T(128)} %param.13) | copy-start | bytes 448
  1026.4 16.2 %copy-start.1 = (f32[1,37,64,16,64]{4,1,2,3,0:T(8,128)S(1)}, f32[1,37,64,16,64]{4,1,2,3,0:T(8,128)}, u32[]{:S(2)}) copy-start(f32[1,37,64,16,64]{4,1,2,3,0:T(8,128)} %copy.42) | copy-start | bytes 29097988
where the time goes:
time: 1080 us; the launch traced here: 1070 us
  local copies, waits for them, and re-layouts  329 us (30%)
  matrix products  283 us (26%)
  blocking collectives  235 us (22%)
  other arithmetic  161 us (15%)
  starting transfers between devices  45 us (4%)
  waiting for transfers between devices  18.7 us (2%)
    dot_general x11, matrix products, dilated(): jnp.einsum('oc,nchw->nohw', kernel[tap_row], stacked, preferred_element_t...  258 us
    concatenate x7, other arithmetic, padded(): array = jnp.concatenate([before, array, after], axis=dim)  132 us
    all_to_all x1, blocking collectives, shards(): lax.all_to_all(logits, 'cols', split_axis=2, concat_axis=3, tiled=True)  122 us
    all_to_all x1, blocking collectives, shards(): lax.all_to_all(strips, ('rows', 'cols'), split_axis=3, concat_axis=2, til...  113 us
    slice x6, local copies, waits for them, and re-layouts, dilated(): widened[:, :, tap_row * dilation:tap_row * dilation + height, tap_col * d...  103 us
    unnamed x51, local copies, waits for them, and re-layouts  63.4 us
    slice x9, local copies, waits for them, and re-layouts, padded(): last = lax.slice_in_dim(array, length - width, length, axis=dim)  47.3 us
    ppermute x8, starting transfers between devices, padded(): before = lax.ppermute(last, axis, up)  34.5 us
  transfers between devices with their start and end apart: 16, of which 7 were waited for; matrix products, arithmetic and copies ran while one was open for 5% of the time, Pallas kernels for 0%

commit v1 on v0

v1 whole, which is shorter than its diff:
```python
import functools

import jax
import jax.numpy as jnp
from jax import lax
from jax.experimental import pallas as pl
from jax.experimental.pallas import tpu as pltpu
from jax.sharding import PartitionSpec as P

BLOCKS = 2
D1 = 4
D2 = 8

FAR = 1 << 20

def chain_kernel(cfg, edge_ref, xt_ref, xi_ref, xb_ref, xh_ref, wa_ref, ba_ref, wb_ref, bb_ref, wo_ref, bo_ref, o_ref, X, I, bias, acc, *xs):
    H, W, C, K, D1, D2, R, LEAD = cfg
    S = W + 64
    halo = 2 * (D1 + D2)
    NB = R * S
    BF = jnp.bfloat16
    F32 = jnp.float32
    T = 256
    def at(row):
        return pl.multiple_of(128 + (row + halo + LEAD) * S, 128)
    X[:, 64 + (LEAD * S):128 + LEAD * S] = xh_ref[0]
    def filler(ref, start):
        def fill(i, _):
            parts = []
            for r in range(R):
                parts += [ref[i * R + r], xh_ref[i * R + r + 1 + start]]
            X[:, pl.ds(at(i * R + start - halo), NB)] = jnp.concatenate(parts, axis=1)
            return 0
        return fill
    lax.fori_loop(0, halo // R, filler(xt_ref, 0), 0)
    lax.fori_loop(0, H // R, filler(xi_ref, halo), 0)
    lax.fori_loop(0, halo // R, filler(xb_ref, halo + H), 0)
    for k in range(2):
        bias[2 * k] = jnp.broadcast_to(ba_ref[k], (C, 128))
        bias[2 * k + 1] = jnp.broadcast_to(bb_ref[k], (C, 128))
    top, bottom, left, right = edge_ref[0], edge_ref[1], edge_ref[2], edge_ref[3]
    lane = lax.broadcasted_iota(jnp.int32, (8, NB), 1)
    col = lane % S
    dead = ((col >= W) & (col < W + 32) & (right > 0)) | ((col >= W + 32) & (left > 0))
    rl = jnp.where(dead, 4 * FAR, lane // S + jnp.where(col >= W + 32, 1, 0))
    first = jnp.where(top > 0, 0, -FAR)
    last = jnp.where(bottom > 0, H, FAR)

    def masked(v, row, t):
        r = rl[:, t:t + T]
        m = (r >= first - row) & (r < last - row)
        return jnp.where(m[None], v.reshape(C // 8, 8, T), 0.0).reshape(C, T)

    def biased(v, i):
        b = bias[i]
        return v + jnp.concatenate([b] * (T // 128), axis=1)

    def conv(src, d, w_ref, k, lo, hi, emit):
        n = d // R
        ring = 2 * n + 1
        total = (hi - lo) // R + 2 * n
        if total % 2:
            lo -= R
            total += 1
        def slot(j):
            return pl.multiple_of(lax.rem(j, ring) * NB, 128)
        def shift(j, xs):
            x = src[:, pl.ds(pl.multiple_of(at(lo - d + j * R) - 128, 128), NB + 256)]
            xs[0:C, :] = pltpu.roll(x, d, 1)[:, 128:128 + NB]
            xs[C:2 * C, :] = pltpu.roll(x, NB + 256 - d, 1)[:, 128:128 + NB]
        def step(j, xs, nxt):
            shift(j + 1, nxt)
            row = lo - d + j * R
            s0, s1, s2 = slot(j), slot(j + ring - n), slot(j + ring - 2 * n)
            for t in range(0, NB, T):
                x = jnp.concatenate([xs[0:C, t:t + T], src[:, pl.ds(at(row) + t, T)], xs[C:2 * C, t:t + T]], axis=0)
                y = jnp.dot(w_ref[k], x, preferred_element_type=F32)
                done = acc[:, pl.ds(s2 + t, T)] + y[2 * C:]
                acc[:, pl.ds(s1 + t, T)] += y[C:2 * C]
                acc[:, pl.ds(s0 + t, T)] = y[:C]
                emit(row - d, t, done)
        shift(0, xs[0])
        def body(i, _):
            step(2 * i, xs[0], xs[1])
            step(2 * i + 1, xs[1], xs[0])
            return 0
        lax.fori_loop(0, total // 2, body, 0)

    for k in range(2):
        edge = halo if k == 0 else D1 + D2
        def emit_a(row, t, v, k=k):
            v = biased(v, 2 * k)
            e = jnp.where(v > 0, v, jnp.exp(v) - 1.0)
            I[:, pl.ds(at(row) + t, T)] = masked(e, row, t).astype(BF)
        conv(X, D1, wa_ref, k, -(edge - D1) - R, H + edge - D1, emit_a)
        def emit_b(row, t, v, k=k):
            v = biased(v, 2 * k + 1) + X[:, pl.ds(at(row) + t, T)].astype(F32)
            if k == 0:
                v = masked(v, row, t)
            X[:, pl.ds(at(row) + t, T)] = v.astype(BF)
        lo = -(edge - D1 - D2) - (R if k == 0 else 0)
        conv(I, D2, wb_ref, k, lo, H + edge - D1 - D2, emit_b)
    bo = jnp.broadcast_to(bo_ref[...], (bo_ref.shape[0], W))
    def project(i, _):
        x = X[:, pl.ds(at(i * R), NB)]
        for r in range(R):
            g = jnp.dot(wo_ref[...], x[:, r * S:r * S + W], preferred_element_type=F32) + bo
            o_ref[i * R + r] = g.astype(BF)
        return 0
    lax.fori_loop(0, H // R, project, 0)

def chain(edge, xt, xi, xb, xh, wa, ba, wb, bb, wo, bo):
    H, C, W = xi.shape
    K = wo.shape[0]
    R = 4
    halo = 2 * (D1 + D2)
    S = W + 64
    LEAD = 2 * halo
    N = 128 + (H + 2 * halo + LEAD) * S + 256 + 2 * R * S
    KP = -(-K // 16) * 16
    wa = wa.reshape(2, 3 * C, 3 * C)
    wb = wb.reshape(2, 3 * C, 3 * C)
    wo = jnp.pad(wo, ((0, KP - K), (0, 0)))
    bo = jnp.pad(bo, (0, KP - K))[:, None]
    vm = pl.BlockSpec(memory_space=pltpu.VMEM)
    return pl.pallas_call(
        functools.partial(chain_kernel, (H, W, C, K, D1, D2, R, LEAD)),
        out_shape=jax.ShapeDtypeStruct((H, KP, W), jnp.bfloat16),
        in_specs=[pl.BlockSpec(memory_space=pltpu.SMEM)] + [vm] * 10,
        out_specs=vm,
        scratch_shapes=[pltpu.VMEM((C, N), jnp.bfloat16), pltpu.VMEM((C, N), jnp.bfloat16), pltpu.VMEM((4, C, 128), jnp.float32),
                        pltpu.VMEM((C, (2 * (max(D1, D2) // R) + 1) * R * S), jnp.float32)]
                        + [pltpu.VMEM((2 * C, R * S), jnp.bfloat16)] * 2,
        compiler_params=pltpu.CompilerParams(vmem_limit_bytes=63000 * 1024),
        name="chain",
    )(edge, xt, xi, xb, xh, wa, ba[:, :, None], wb, bb[:, :, None], wo, bo)[:, :K]


def neighbours(first, last, axis):
    peers = lax.axis_size(axis)
    up = [(i, i + 1) for i in range(peers - 1)]
    down = [(j, i) for i, j in up]
    return lax.ppermute(last, axis, up), lax.ppermute(first, axis, down)


def shards(pair_maps, conv_a, bias_a, conv_b, bias_b, out_weight, out_bias):
    halo = BLOCKS * (D1 + D2)
    rows, cols = lax.axis_size("rows"), lax.axis_size("cols")
    field = jnp.transpose(pair_maps[0], (1, 0, 2))
    above, below = neighbours(field[:halo], field[-halo:], "rows")
    west = jnp.concatenate([v[:, :, :halo] for v in (above, field, below)], axis=0)
    east = jnp.concatenate([v[:, :, -halo:] for v in (above, field, below)], axis=0)
    left, right = neighbours(west, east, "cols")
    side = jnp.concatenate(
        [
            jnp.pad(right, ((1, 0), (0, 0), (0, 64 - 2 * halo))),
            jnp.pad(left, ((0, 1), (0, 0), (0, 0))),
        ],
        axis=2,
    )
    r, c = lax.axis_index("rows"), lax.axis_index("cols")
    edge = jnp.stack([r == 0, r == rows - 1, c == 0, c == cols - 1]).astype(jnp.int32)
    logits = chain(edge, above, field, below, side, conv_a, bias_a, conv_b, bias_b, out_weight, out_bias)
    logits = jnp.transpose(logits, (1, 0, 2))[None]
    strips = lax.all_to_all(logits, "cols", split_axis=2, concat_axis=3, tiled=True)
    flipped = lax.all_to_all(strips, ("rows", "cols"), split_axis=3, concat_axis=2, tiled=True)
    mirrored = jnp.swapaxes(flipped, 2, 3)
    symmetric = (strips.astype(jnp.float32) + mirrored.astype(jnp.float32)) * 0.5
    return symmetric - jnp.log(jnp.sum(jnp.exp(symmetric), axis=1, keepdims=True))


def solution(mesh):
    in_specs = (P("crops", None, "rows", "cols"), P(), P(), P(), P(), P(), P())
    out_specs = P("crops", None, ("rows", "cols"), None)
    body = jax.shard_map(shards, mesh=mesh, in_specs=in_specs, out_specs=out_specs, check_vma=False)

    def run(*args):
        with jax.sharding.use_abstract_mesh(mesh.abstract_mesh):
            return body(*args)

    return run
```

time: 1080 us -> 557 us (0.52)
  matrix products: 283 us -> 0 us
  local copies, waits for them, and re-layouts: 329 us -> 138 us
  other arithmetic: 161 us -> 44 us
  Pallas kernels: 0 us -> 108 us
  starting transfers between devices: 45 us -> 12.3 us
    dot_general x12 -> x0, matrix products: 283 us -> none  [the longest x11 258 us: dilated(): jnp.einsum('oc,nchw->nohw', kernel[tap_row], stacked, preferred_element_t...]
    slice x22 -> x10, local copies, waits for them, and re-layouts: 177 us -> 29.7 us  [the longest x6 17.8 us: shards(): v[:, :, :halo]]
    concatenate x7 -> x3, other arithmetic: 132 us -> 14.3 us  [the longest x1 8.54 us: shards(): jnp.concatenate([jnp.pad(right, ((1, 0), (0, 0), (0, 64 - 2 * halo))), jn...]
    pallas_call x0 -> x1, Pallas kernels: none -> 108 us  [chain(): pl.pallas_call(functools.partial(chain_kernel, (H, W, C, K, D1, D2, R, LE...]
    ppermute x16 -> x4, starting transfers between devices: 45 us -> 12.3 us  [neighbours(): return (lax.ppermute(last, axis, up), lax.ppermute(first, axis, down))]
    ppermute x8 -> x2, local copies, waits for them, and re-layouts: 40.3 us -> 13.1 us  [neighbours(): return (lax.ppermute(last, axis, up), lax.ppermute(first, axis, down))]
    unnamed x51 -> x17, local copies, waits for them, and re-layouts: 63.4 us -> 43 us
  transfers between devices with their start and end apart: 16 -> 4, of which waited for: 7 -> 1; matrix products, arithmetic and copies ran while one was open for 5% -> 6% of each run, Pallas kernels for 0% -> 0%
where the time goes in v1:
time: 557 us; the launch traced here: 554 us
  blocking collectives  234 us (42%)
  local copies, waits for them, and re-layouts  138 us (25%)
  Pallas kernels  108 us (19%)
  other arithmetic  44 us (8%)
  waiting for transfers between devices  17.3 us (3%)
  starting transfers between devices  12.3 us (2%)
    all_to_all x1, blocking collectives, shards(): lax.all_to_all(logits, 'cols', split_axis=2, concat_axis=3, tiled=True)  121 us
    all_to_all x1, blocking collectives, shards(): lax.all_to_all(strips, ('rows', 'cols'), split_axis=3, concat_axis=2, til...  113 us
    pallas_call x1, Pallas kernels, chain(): pl.pallas_call(functools.partial(chain_kernel, (H, W, C, K, D1, D2, R, LE...  108 us
    unnamed x17, local copies, waits for them, and re-layouts  43 us
    convert_element_type x1, local copies, waits for them, and re-layouts, shards(): mirrored.astype(jnp.float32)  18.3 us
    slice x6, local copies, waits for them, and re-layouts, shards(): v[:, :, :halo]  17.8 us
    ppermute x4, waiting for transfers between devices, neighbours(): return (lax.ppermute(last, axis, up), lax.ppermute(first, axis, down))  17.3 us
    sub x1, local copies, waits for them, and re-layouts, shards(): symmetric - jnp.log(jnp.sum(jnp.exp(symmetric), axis=1, keepdims=True))  15.6 us
  transfers between devices with their start and end apart: 4, of which 1 were waited for; matrix products, arithmetic and copies ran while one was open for 6% of the time, Pallas kernels for 0%

profile of v1, /device:TPU:0, one launch (start us, length us, event | category | flops | bytes accessed | tf_op | source)
XLA Modules:
  0.0 554.5 jit_solution(15320048812172935751)
XLA Ops:
  0.0 11.5 %copy.31 = bf16[1,64,256,256]{3,1,2,0:T(8,128)(2,1)} copy(bf16[1,64,256,256]{3,2,1,0:T(8,128)(2,1)} %param.7) | data formatting | bytes 16777216 | tf_op args[0]
  11.5 2.7 fusion.5
  14.3 1.3 collective-permute-start.1
  15.6 3.1 collective-permute-start
  18.7 6.3 %fusion.4 = (bf16[256,64,24]{2,1,0:T(8,128)(2,1)}, bf16[256,64,24]{2,1,0:T(8,128)(2,1)}) fusion(bf16[256,64,256]{2,1,0:T(8,128)(2,1)} %bitcast.40), kind=kLoop, calls=%fused_computation.14 | loop fusion | bytes 3145728 | tf_op jit(solution)/shard_map/slice | solution.py:151
  25.0 4.8 copy.16
  29.8 4.8 copy.20
  34.6 0.0 collective-permute-done.1.xb_ref
  34.7 0.0 copy-start.1
  34.7 1.2 fusion.7
  35.8 2.2 copy.17
  38.0 2.1 copy.21
  40.2 0.0 collective-permute-done.xt_ref
  40.2 1.2 fusion.6
  41.4 2.1 copy.15
  43.5 2.2 copy.19
  45.7 2.9 pad_maximum_fusion
  48.6 1.3 collective-permute-start.2
  49.8 2.9 pad_maximum_fusion.1
  52.7 0.0 copy-done.1
  52.7 6.7 %collective-permute-start.3 = (bf16[304,64,24]{0,2,1:T(8,128)(2,1)}, bf16[304,64,24]{0,2,1:T(8,128)(2,1)}, u32[]{:S(2)}, u32[]{:S(2)}) collective-permute-start(bf16[304,64,24]{0,2,1:T(8,128)(2,1)} %pad_maximum_fusion.1), channel_id=1, source_target_pairs={{0,1},{1,2},{2,3},{4,5},{5,6},{6,7},{8,9},{9,10},{10,11},{12,13},{... | collective-permute-start | bytes 2801672 | tf_op jit(solution)/shard_map/ppermute | solution.py:143
  59.4 0.0 copy-done.6
  59.4 0.7 copy.25.bo_ref
  60.1 0.0 copy-done.4
  60.1 0.7 copy.23.ba_ref
  60.8 0.0 copy-done.5
  60.8 0.7 copy.24.bb_ref
  61.6 0.0 copy-done.3
  61.6 0.6 pad.18.wo_ref
  62.2 0.6 add_convert_fusion.edge_ref
  62.8 17.3 %collective-permute-done.2 = bf16[304,64,24]{0,2,1:T(8,128)(2,1)} collective-permute-done((bf16[304,64,24]{0,2,1:T(8,128)(2,1)}, bf16[304,64,24]{0,2,1:T(8,128)(2,1)}, u32[]{:S(2)}, u32[]{:S(2)}) %collective-permute-start.2) | collective-permute-done | bytes 933920 | tf_op jit(solution)/shard_map/ppermute | solution.py:143
  80.1 6.5 %copy.18 = bf16[304,64,24]{2,1,0:T(8,128)(2,1)} copy(bf16[304,64,24]{0,2,1:T(8,128)(2,1)} %collective-permute-done.2) | data formatting | bytes 1867776 | tf_op jit(solution)/shard_map/ppermute | solution.py:143
  86.6 0.0 collective-permute-done.3
  86.6 6.6 %copy.22 = bf16[304,64,24]{2,1,0:T(8,128)(2,1)} copy(bf16[304,64,24]{0,2,1:T(8,128)(2,1)} %collective-permute-done.3) | data formatting | bytes 1867776 | tf_op jit(solution)/shard_map/ppermute | solution.py:143
  93.2 8.5 %fusion.3.xh_ref = bf16[305,64,64]{2,1,0:T(8,128)(2,1)} fusion(bf16[304,64,24]{2,1,0:T(8,128)(2,1)} %copy.22, bf16[304,64,24]{2,1,0:T(8,128)(2,1)} %copy.18), kind=kLoop, calls=%fused_computation.9 | loop fusion | flops 9994240 | bytes 4366336 | tf_op jit(solution)/shard_map/concatenate | solution.py:154
  101.8 108.3 %chain.1 = bf16[256,48,256]{2,1,0:T(8,128)(2,1)} custom-call(s32[4]{0:T(128)} %add_convert_fusion.edge_ref, bf16[24,64,256]{2,1,0:T(8,128)(2,1)} %copy-done.2, bf16[256,64,256]{2,1,0:T(8,128)(2,1)} %bitcast.41, bf16[24,64,256]{2,1,0:T(8,128)(2,1)} %copy-done.1, bf16[305,64,64]{2,1,0:T(8,128)(2,1)} %fusion.3.xh_ref, bf16[2,192,192]{2,1,0:T(8,128)(2,1)} %bitcast.44, ...), custom_call_target="tpu_custom_call" | custom-call | tf_op jit(solution)/shard_map/chain/pallas_call | solution.py:126
  210.0 2.9 slice_bitcast_fusion
  212.9 121.0 %all_to_all.27 = bf16[1,37,256,256]{3,1,0,2:T(8,128)(2,1)} all-to-all(bf16[1,37,256,256]{3,1,0,2:T(8,128)(2,1)S(1)} %slice_bitcast_fusion), channel_id=1, replica_groups=mesh['crops'=2,'rows'=4,'cols'=4] {'cols'}, dimensions={2} | all-to-all | bytes 9699328 | tf_op jit(solution)/shard_map/all_to_all | solution.py:165
  333.9 13.1 %copy.27 = bf16[1,37,64,4,256]{2,1,4,3,0:T(8,128)(2,1)} copy(bf16[1,37,64,4,256]{4,1,2,3,0:T(8,128)(2,1)} %bitcast.43) | data formatting | bytes 9699328 | tf_op jit(solution)/shard_map/all_to_all | solution.py:165
  347.0 14.8 %reshape.35 = bf16[16,2,75776]{2,1,0:T(2,128)(2,1)} reshape(bf16[1024,1,37,64]{3,2,1,0:T(8,128)(2,1)} %bitcast.36) | data formatting | bytes 9699328
  361.8 113.0 %all_to_all.28 = bf16[16,2,75776]{2,1,0:T(2,128)(2,1)} all-to-all(bf16[16,2,75776]{2,1,0:T(2,128)(2,1)} %reshape.35), channel_id=1, replica_groups=mesh['crops'=2,'rows'=4,'cols'=4] {'rows','cols'}, dimensions={0} | all-to-all | bytes 9699328 | tf_op jit(solution)/shard_map/all_to_all | solution.py:166
  474.8 16.0 %reshape.36 = bf16[1024,1,37,64]{3,2,1,0:T(8,128)(2,1)} reshape(bf16[16,2,75776]{2,1,0:T(2,128)(2,1)} %all_to_all.28) | data formatting | bytes 9699328
  490.7 18.3 %copy.28 = f32[1,37,64,16,64]{4,1,2,3,0:T(8,128)} copy(bf16[1,37,64,16,64]{2,1,4,3,0:T(8,128)(2,1)} %bitcast.42) | data formatting | bytes 14548992 | tf_op jit(solution)/shard_map/convert_element_type | solution.py:168
  509.1 15.5 %exponential_reduce_fusion = f32[64,1024]{0,1:T(8,128)S(1)} fusion(f32[1,37,64,1024]{2,1,0,3:T(8,128)} %bitcast.34, bf16[1,37,64,1024]{2,1,0,3:T(8,128)(2,1)} %bitcast.37), kind=kLoop, calls=%fused_computation | loop fusion | flops 9633792 | bytes 14811136 | tf_op jit(solution)/shard_map/reduce_sum | solution.py:169
  524.5 0.1 log.8
  524.6 0.7 copy-done
  525.3 13.6 %fusion = f32[1,37,64,1024]{2,1,0,3:T(8,128)} fusion(f32[1,37,64,1024]{2,1,0,3:T(8,128)S(1)} %bitcast.35, bf16[1,37,64,1024]{2,1,0,3:T(8,128)(2,1)} %bitcast.38, f32[64,1024]{0,1:T(8,128)S(1)} %log.8), kind=kLoop, calls=%fused_computation.2 | loop fusion | flops 9699328 | bytes 24510464 | tf_op jit(solution)/shard_map/sub | solution.py:169
  538.9 15.6 %copy.29 = f32[1,37,64,1024]{3,2,1,0:T(8,128)} copy(f32[1,37,64,1024]{2,1,0,3:T(8,128)} %fusion) | data formatting | bytes 19398656 | tf_op jit(solution)/shard_map/sub | solution.py:169
  (8 shorter events, 0.0 us)
Async XLA Ops:
  14.3 20.4 %collective-permute-start.1 = (bf16[24,64,256]{2,1,0:T(8,128)(2,1)}, bf16[24,64,256]{2,1,0:T(8,128)(2,1)S(1)}, u32[]{:S(2)}, u32[]{:S(2)}) collective-permute-start(bf16[24,64,256]{2,1,0:T(8,128)(2,1)} %get-tuple-element.7), channel_id=1, source_target_pairs={{4,0},{8,4},{12,8},{5,1},{9,5},{13,9},{6,2},{10,6},{14,10},{7,3},{... | collective-permute-start | bytes 2359304 | tf_op jit(solution)/shard_map/ppermute | solution.py:143
  15.6 24.6 %collective-permute-start = (bf16[24,64,256]{2,1,0:T(8,128)(2,1)}, bf16[24,64,256]{2,1,0:T(8,128)(2,1)S(1)}, u32[]{:S(2)}, u32[]{:S(2)}) collective-permute-start(bf16[24,64,256]{2,1,0:T(8,128)(2,1)} %get-tuple-element.8), channel_id=1, source_target_pairs={{0,4},{4,8},{8,12},{1,5},{5,9},{9,13},{2,6},{6,10},{10,14},{3,7},{... | collective-permute-start | bytes 2359304 | tf_op jit(solution)/shard_map/ppermute | solution.py:143
  34.7 18.1 %copy-start.1 = (bf16[24,64,256]{2,1,0:T(8,128)(2,1)}, bf16[24,64,256]{2,1,0:T(8,128)(2,1)S(1)}, u32[]{:S(2)}) copy-start(bf16[24,64,256]{2,1,0:T(8,128)(2,1)S(1)} %collective-permute-done.1.xb_ref) | copy-start | bytes 2359300
  35.8 23.6 %copy-start.6 = (f32[37]{0:T(128)S(1)}, f32[37]{0:T(128)}, u32[]{:S(2)}) copy-start(f32[37]{0:T(128)} %param.13) | copy-start | bytes 448
  35.8 24.3 %copy-start.4 = (f32[2,64]{1,0:T(2,128)S(1)}, f32[2,64]{1,0:T(2,128)}, u32[]{:S(2)}) copy-start(f32[2,64]{1,0:T(2,128)} %param.9) | copy-start | bytes 1540
  35.8 25.0 %copy-start.5 = (f32[2,64]{1,0:T(2,128)S(1)}, f32[2,64]{1,0:T(2,128)}, u32[]{:S(2)}) copy-start(f32[2,64]{1,0:T(2,128)} %param.11) | copy-start | bytes 1540
  38.0 23.5 %copy-start.3 = (bf16[37,64]{1,0:T(8,128)(2,1)S(1)}, bf16[37,64]{1,0:T(8,128)(2,1)}, u32[]{:S(2)}) copy-start(bf16[37,64]{1,0:T(8,128)(2,1)} %param.12) | copy-start | bytes 14212
  40.2 46.4 %copy-start.2 = (bf16[24,64,256]{2,1,0:T(8,128)(2,1)}, bf16[24,64,256]{2,1,0:T(8,128)(2,1)S(1)}, u32[]{:S(2)}) copy-start(bf16[24,64,256]{2,1,0:T(8,128)(2,1)S(1)} %collective-permute-done.xt_ref) | copy-start | bytes 2359300
  48.6 31.5 %collective-permute-start.2 = (bf16[304,64,24]{0,2,1:T(8,128)(2,1)}, bf16[304,64,24]{0,2,1:T(8,128)(2,1)}, u32[]{:S(2)}, u32[]{:S(2)}) collective-permute-start(bf16[304,64,24]{0,2,1:T(8,128)(2,1)} %pad_maximum_fusion), channel_id=1, source_target_pairs={{1,0},{2,1},{3,2},{5,4},{6,5},{7,6},{9,8},{10,9},{11,10},{13,12},{... | collective-permute-start | bytes 2801672 | tf_op jit(solution)/shard_map/ppermute | solution.py:143
  52.7 33.9 %collective-permute-start.3 = (bf16[304,64,24]{0,2,1:T(8,128)(2,1)}, bf16[304,64,24]{0,2,1:T(8,128)(2,1)}, u32[]{:S(2)}, u32[]{:S(2)}) collective-permute-start(bf16[304,64,24]{0,2,1:T(8,128)(2,1)} %pad_maximum_fusion.1), channel_id=1, source_target_pairs={{0,1},{1,2},{2,3},{4,5},{5,6},{6,7},{8,9},{9,10},{10,11},{12,13},{... | collective-permute-start | bytes 2801672 | tf_op jit(solution)/shard_map/ppermute | solution.py:143
  509.1 16.2 %copy-start = (f32[1,37,64,16,64]{4,1,2,3,0:T(8,128)S(1)}, f32[1,37,64,16,64]{4,1,2,3,0:T(8,128)}, u32[]{:S(2)}) copy-start(f32[1,37,64,16,64]{4,1,2,3,0:T(8,128)} %copy.28) | copy-start | bytes 29097988
